TPU v7x, 32 devices: a whole 2x2x4 slice. The times are simulated.
32 devices in a mesh: fsdp: 8 (over z, x), tp: 4 (over y, core).
Axes of the slice: x: 2, y: 2, z: 4, core: 2. Of those that a mesh axis runs over, the one named last changes fastest.
Arguments:
- inputs: bfloat16 [32768, 512], P(('fsdp', 'tp')), may hold values from -6 to 6
- segments: int32 [8, 4096], P('fsdp', 'tp'), may hold values from 0 to 20, as said below
- out_grad: bfloat16 [32768, 512], P(('fsdp', 'tp')), may hold values from -6 to 6
- first_gain: bfloat16 [512], replicated, may hold values from 0.5 to 1.5
- first_shift: bfloat16 [512], replicated, may hold values from -3 to 3
- qkv_weight: bfloat16 [512, 3, 512], P('fsdp', None, 'tp'), may hold values from -0.375 to 0.375
- qv_bias: bfloat16 [2, 512], replicated, may hold values from -3 to 3
- out_weight: bfloat16 [512, 512], P('tp', 'fsdp'), may hold values from -1 to 1
- out_bias: bfloat16 [512], replicated, may hold values from -3 to 3
- second_gain: bfloat16 [512], replicated, may hold values from 0.5 to 1.5
- second_shift: bfloat16 [512], replicated, may hold values from -3 to 3
- fc_weight: bfloat16 [512, 2048], P('fsdp', 'tp'), may hold values from -0.25 to 0.25
- fc_bias: bfloat16 [2048], replicated, may hold values from -3 to 3
- proj_weight: bfloat16 [2048, 512], P('tp', 'fsdp'), may hold values from -0.125 to 0.125
- proj_bias: bfloat16 [512], replicated, may hold values from -3 to 3
Outputs:
- layer_out: bfloat16 [32768, 512], P(('fsdp', 'tp'))
- input_grad: bfloat16 [32768, 512], P(('fsdp', 'tp'))
- first_gain_grad: float32 [512], replicated
- first_shift_grad: float32 [512], replicated
- qkv_weight_grad: float32 [512, 3, 512], P('fsdp', None, 'tp')
- qv_bias_grad: float32 [2, 512], replicated
- out_weight_grad: float32 [512, 512], P('tp', 'fsdp')
- out_bias_grad: float32 [512], replicated
- second_gain_grad: float32 [512], replicated
- second_shift_grad: float32 [512], replicated
- fc_weight_grad: float32 [512, 2048], P('fsdp', 'tp')
- fc_bias_grad: float32 [2048], replicated
- proj_weight_grad: float32 [2048, 512], P('tp', 'fsdp')
- proj_bias_grad: float32 [512], replicated
Inputs may be any that keep to these rules, and one draw needn't show every extreme that they name: `segments`: along each sequence the numbers start at 1 and rise by one from document to document; each document has 200 to 2000 tokens, and in one sequence every document has exactly 200; 0 marks padding, which only follows the last whole document of a sequence.
All inputs are finite; a program needn't handle non-finite values.
Results may differ from a plain program's by a relative error of at most 0.018.
The roundings to bfloat16 on the way count: a program that leaves them out, or rounds other values in their place, can miss the bound.
Values may be sent and summed in bfloat16 or wider, within the bound.
A program may use at most 128 MiB of HBM per device.

v0:
```python
import jax
import jax.numpy as jnp
from jax import lax
from jax.sharding import PartitionSpec as P

HD = 64
FF = 2048
epsilon = 1e-05
gelu_slope = 1.702
masked_score = -1e30


def split_up(value, dim, peers):
    dims = value.shape
    pieces = value.reshape(*dims[:dim], peers, dims[dim] // peers, *dims[dim + 1 :])
    return jnp.moveaxis(pieces, dim, 0)


def sent_and_summed(value, axis, dim):
    pieces = split_up(value, dim, lax.axis_size(axis))
    arrived = lax.all_to_all(pieces, axis, split_axis=0, concat_axis=0, tiled=True)
    return arrived.astype(jnp.float32).sum(axis=0)


def layer_norm(values_in, gain_vec, shift_vec):
    mean_row = jnp.mean(values_in, axis=-1, keepdims=True)
    centred = values_in - mean_row
    inverse = lax.rsqrt(jnp.mean(centred * centred, axis=-1, keepdims=True) + epsilon)
    normed = centred * inverse
    return (normed * gain_vec + shift_vec, normed, inverse)


def norm_back(grad_out, normed, inverse, gain_vec):
    scaled = grad_out * gain_vec
    grad_in = inverse * (
        scaled
        - jnp.mean(scaled, axis=-1, keepdims=True)
        - normed * jnp.mean(scaled * normed, axis=-1, keepdims=True)
    )
    return (grad_in, jnp.sum(grad_out * normed, axis=0), jnp.sum(grad_out, axis=0))


def allowed(seg_query, pos_query, seg_key, pos_key):
    same_doc = seg_query[:, None] == seg_key[None, :]
    causal = pos_key[None, :] <= pos_query[:, None]
    living = (seg_query[:, None] != 0) | (pos_key[None, :] == pos_query[:, None])
    return same_doc & causal & living


def attend(queries, keys_all, values_all, seg_all, block_rows):
    seq_rows, heads_here, head_size = queries.shape
    blocks = seq_rows // block_rows
    positions = jnp.arange(seq_rows, dtype=jnp.int32)
    scale_factor = head_size ** (-0.5)

    def one_block(pieces):
        q_blk, seg_blk, pos_blk = pieces
        scores = (
            jnp.einsum("qhe,khe->hqk", q_blk, keys_all, preferred_element_type=jnp.float32)
            * scale_factor
        )
        allowed_mask = allowed(seg_blk, pos_blk, seg_all, positions)
        scores = jnp.where(allowed_mask[None], scores, masked_score)
        row_max = jnp.max(scores, axis=-1, keepdims=True)
        exp_scores = jnp.exp(scores - row_max)
        row_sum = jnp.sum(exp_scores, axis=-1, keepdims=True)
        softmax_w = (exp_scores / row_sum).astype(jnp.bfloat16)
        block_out = jnp.einsum(
            "hqk,khe->qhe", softmax_w, values_all, preferred_element_type=jnp.float32
        )
        return (block_out, (row_max + jnp.log(row_sum))[..., 0])

    block_outs, log_norm = lax.map(
        one_block,
        (
            queries.reshape(blocks, block_rows, heads_here, head_size),
            seg_all.reshape(blocks, block_rows),
            positions.reshape(blocks, block_rows),
        ),
    )
    return (block_outs.reshape(seq_rows, heads_here, head_size), log_norm)


def attend_back(queries, keys_all, values_all, grad_out, raw_out, log_norm, seg_all, block_rows):
    seq_rows, heads_here, head_size = queries.shape
    blocks = seq_rows // block_rows
    positions = jnp.arange(seq_rows, dtype=jnp.int32)
    scale_factor = head_size ** (-0.5)
    row_dot = jnp.sum(grad_out.astype(jnp.float32) * raw_out, axis=-1)

    def one_block(running, pieces):
        grad_keys, grad_values = running
        q_blk, g_blk, dot_blk, norm_blk, seg_blk, pos_blk = pieces
        scores = (
            jnp.einsum("qhe,khe->hqk", q_blk, keys_all, preferred_element_type=jnp.float32)
            * scale_factor
        )
        allowed_mask = allowed(seg_blk, pos_blk, seg_all, positions)
        scores = jnp.where(allowed_mask[None], scores, masked_score)
        softmax_f = jnp.exp(scores - norm_blk[..., None])
        grad_soft = jnp.einsum(
            "qhe,khe->hqk", g_blk, values_all, preferred_element_type=jnp.float32
        )
        grad_scores = (softmax_f * (grad_soft - dot_blk.T[..., None]) * scale_factor).astype(
            jnp.bfloat16
        )
        grad_q = jnp.einsum(
            "hqk,khe->qhe", grad_scores, keys_all, preferred_element_type=jnp.float32
        )
        grad_keys = grad_keys + jnp.einsum(
            "hqk,qhe->khe", grad_scores, q_blk, preferred_element_type=jnp.float32
        )
        grad_values = grad_values + jnp.einsum(
            "hqk,qhe->khe",
            softmax_f.astype(jnp.bfloat16),
            g_blk,
            preferred_element_type=jnp.float32,
        )
        return ((grad_keys, grad_values), grad_q)

    zero_state = jnp.zeros((seq_rows, heads_here, head_size), jnp.float32)
    (grad_keys, grad_values), grad_queries = lax.scan(
        one_block,
        (zero_state, zero_state),
        (
            queries.reshape(blocks, block_rows, heads_here, head_size),
            grad_out.reshape(blocks, block_rows, heads_here, head_size),
            row_dot.reshape(blocks, block_rows, heads_here),
            log_norm,
            seg_all.reshape(blocks, block_rows),
            positions.reshape(blocks, block_rows),
        ),
    )
    return (grad_queries.reshape(seq_rows, heads_here, head_size), grad_keys, grad_values)


def local(
    inputs,
    segments,
    out_grad,
    first_gain,
    first_shift,
    qkv_weight,
    qv_bias,
    out_weight,
    out_bias,
    second_gain,
    second_shift,
    fc_weight,
    fc_bias,
    proj_weight,
    proj_bias,
):
    tp_index = lax.axis_index("tp")
    qkv_full, out_full, fc_full, proj_full = (
        lax.all_gather(qkv_weight, "fsdp", axis=0, tiled=True),
        lax.all_gather(out_weight, "fsdp", axis=1, tiled=True),
        lax.all_gather(fc_weight, "fsdp", axis=0, tiled=True),
        lax.all_gather(proj_weight, "fsdp", axis=1, tiled=True),
    )
    model_width = inputs.shape[1]
    head_cols = qkv_full.shape[2]
    hidden_cols = fc_full.shape[1]
    heads_here = head_cols // HD
    resid_in = inputs.astype(jnp.float32)
    normed_one, hat_one, inv_one = layer_norm(
        resid_in, first_gain.astype(jnp.float32), first_shift.astype(jnp.float32)
    )
    lowered_one = normed_one.astype(jnp.bfloat16)
    seq_normed, seg_rows = (
        lax.all_gather(lowered_one, "tp", axis=0, tiled=True),
        lax.all_gather(segments, "tp", axis=1, tiled=True),
    )
    seg_all = seg_rows[0]
    seq_rows = seq_normed.shape[0]
    block_rows = min(512, seq_rows)
    projected = jnp.einsum("sd,dje->sje", seq_normed, qkv_full, preferred_element_type=jnp.float32)
    bias_here = lax.dynamic_slice_in_dim(qv_bias, tp_index * head_cols, head_cols, 1).astype(
        jnp.float32
    )
    queries = (
        (projected[:, 0] + bias_here[0]).astype(jnp.bfloat16).reshape(seq_rows, heads_here, HD)
    )
    keys_all = projected[:, 1].astype(jnp.bfloat16).reshape(seq_rows, heads_here, HD)
    values_all = (
        (projected[:, 2] + bias_here[1]).astype(jnp.bfloat16).reshape(seq_rows, heads_here, HD)
    )
    live_rows = (seg_all != 0).astype(jnp.float32)
    raw_out, log_norm = attend(queries, keys_all, values_all, seg_all, block_rows)
    attn_low = (
        (raw_out * live_rows[:, None, None]).astype(jnp.bfloat16).reshape(seq_rows, head_cols)
    )
    attn_sum = lax.psum_scatter(
        jnp.dot(attn_low, out_full, preferred_element_type=jnp.float32).astype(jnp.bfloat16),
        "tp",
        scatter_dimension=0,
        tiled=True,
    ).astype(jnp.float32)
    hidden = resid_in + attn_sum + out_bias.astype(jnp.float32)
    normed_two, hat_two, inv_two = layer_norm(
        hidden, second_gain.astype(jnp.float32), second_shift.astype(jnp.float32)
    )
    lowered_two = normed_two.astype(jnp.bfloat16)
    mlp_in = lax.all_gather(lowered_two, "tp", axis=0, tiled=True)
    fc_bias_here = lax.dynamic_slice_in_dim(fc_bias, tp_index * hidden_cols, hidden_cols, 0)
    pre_act = jnp.dot(mlp_in, fc_full, preferred_element_type=jnp.float32) + fc_bias_here.astype(
        jnp.float32
    )
    sigmoid_pre = jax.nn.sigmoid(gelu_slope * pre_act)
    act_low = (pre_act * sigmoid_pre).astype(jnp.bfloat16)
    mlp_sum = lax.psum_scatter(
        jnp.dot(act_low, proj_full, preferred_element_type=jnp.float32).astype(jnp.bfloat16),
        "tp",
        scatter_dimension=0,
        tiled=True,
    ).astype(jnp.float32)
    grad_rows = lax.all_gather(out_grad, "tp", axis=0, tiled=True)
    layer_out = (hidden + mlp_sum + proj_bias.astype(jnp.float32)).astype(jnp.bfloat16)
    proj_grad = jnp.einsum("sf,sd->fd", act_low, grad_rows, preferred_element_type=jnp.float32)
    grad_act = jnp.einsum("sd,fd->sf", grad_rows, proj_full, preferred_element_type=jnp.float32)
    grad_pre = grad_act * (sigmoid_pre + gelu_slope * pre_act * sigmoid_pre * (1.0 - sigmoid_pre))
    grad_pre_low = grad_pre.astype(jnp.bfloat16)
    fc_grad = jnp.einsum("sd,sf->df", mlp_in, grad_pre_low, preferred_element_type=jnp.float32)
    fc_bias_part = jnp.sum(grad_pre_low.astype(jnp.float32), axis=0)
    grad_normed_two = lax.psum_scatter(
        jnp.einsum("sf,df->sd", grad_pre_low, fc_full, preferred_element_type=jnp.float32).astype(
            jnp.bfloat16
        ),
        "tp",
        scatter_dimension=0,
        tiled=True,
    ).astype(jnp.float32)
    fc_bias_full = lax.dynamic_update_slice_in_dim(
        jnp.zeros((FF,), jnp.float32), fc_bias_part, tp_index * hidden_cols, 0
    )
    resid_grad = out_grad.astype(jnp.float32)
    grad_hidden_ln, second_gain_part, second_shift_part = norm_back(
        grad_normed_two, hat_two, inv_two, second_gain.astype(jnp.float32)
    )
    grad_hidden = resid_grad + grad_hidden_ln
    grad_hidden_low = grad_hidden.astype(jnp.bfloat16)
    out_bias_part = jnp.sum(grad_hidden_low.astype(jnp.float32), axis=0)
    proj_bias_part = jnp.sum(resid_grad, axis=0)
    seq_grad = lax.all_gather(grad_hidden_low, "tp", axis=0, tiled=True)
    out_w_grad = jnp.einsum("sc,sd->cd", attn_low, seq_grad, preferred_element_type=jnp.float32)
    grad_attn = jnp.einsum("sd,cd->sc", seq_grad, out_full, preferred_element_type=jnp.float32)
    grad_attn_low = (
        grad_attn.astype(jnp.bfloat16).reshape(seq_rows, heads_here, HD)
        * live_rows.astype(jnp.bfloat16)[:, None, None]
    )
    grad_q, grad_k, grad_v = attend_back(
        queries, keys_all, values_all, grad_attn_low, raw_out, log_norm, seg_all, block_rows
    )
    grad_qkv = (
        jnp.stack([grad_q, grad_k, grad_v], axis=1)
        .astype(jnp.bfloat16)
        .reshape(seq_rows, 3, head_cols)
    )
    qkv_w_grad = jnp.einsum("sd,sje->dje", seq_normed, grad_qkv, preferred_element_type=jnp.float32)
    qv_part = jnp.sum(grad_qkv[:, 0::2].astype(jnp.float32), axis=0)
    grad_normed_one = lax.psum_scatter(
        jnp.einsum("sje,dje->sd", grad_qkv, qkv_full, preferred_element_type=jnp.float32).astype(
            jnp.bfloat16
        ),
        "tp",
        scatter_dimension=0,
        tiled=True,
    ).astype(jnp.float32)
    qv_full = lax.dynamic_update_slice_in_dim(
        jnp.zeros((2, model_width), jnp.float32), qv_part, tp_index * head_cols, 1
    )
    grad_in_ln, first_gain_part, first_shift_part = norm_back(
        grad_normed_one, hat_one, inv_one, first_gain.astype(jnp.float32)
    )
    input_grad = (grad_hidden + grad_in_ln).astype(jnp.bfloat16)
    qkv_w_grad, out_w_grad, fc_grad, proj_grad = (
        sent_and_summed(qkv_w_grad.astype(jnp.bfloat16), "fsdp", 0),
        sent_and_summed(out_w_grad.astype(jnp.bfloat16), "fsdp", 1),
        sent_and_summed(fc_grad.astype(jnp.bfloat16), "fsdp", 0),
        sent_and_summed(proj_grad.astype(jnp.bfloat16), "fsdp", 1),
    )
    (
        first_gain_grad,
        first_shift_grad,
        qv_bias_grad,
        out_bias_grad,
        second_gain_grad,
        second_shift_grad,
        fc_bias_grad,
        proj_bias_grad,
    ) = lax.psum(
        (
            first_gain_part,
            first_shift_part,
            qv_full,
            out_bias_part,
            second_gain_part,
            second_shift_part,
            fc_bias_full,
            proj_bias_part,
        ),
        ("fsdp", "tp"),
    )
    return (
        layer_out,
        input_grad,
        first_gain_grad,
        first_shift_grad,
        qkv_w_grad,
        qv_bias_grad,
        out_w_grad,
        out_bias_grad,
        second_gain_grad,
        second_shift_grad,
        fc_grad,
        fc_bias_grad,
        proj_grad,
        proj_bias_grad,
    )


def solution(mesh):
    return jax.shard_map(
        local,
        mesh=mesh,
        in_specs=(
            P(("fsdp", "tp"), None),
            P("fsdp", "tp"),
            P(("fsdp", "tp"), None),
            P(),
            P(),
            P("fsdp", None, "tp"),
            P(),
            P("tp", "fsdp"),
            P(),
            P(),
            P(),
            P("fsdp", "tp"),
            P(),
            P("tp", "fsdp"),
            P(),
        ),
        out_specs=(
            P(("fsdp", "tp"), None),
            P(("fsdp", "tp"), None),
            P(),
            P(),
            P("fsdp", None, "tp"),
            P(),
            P("tp", "fsdp"),
            P(),
            P(),
            P(),
            P("fsdp", "tp"),
            P(),
            P("tp", "fsdp"),
            P(),
        ),
        check_vma=False,
    )
```

profile of v0, /device:TPU:0, one launch (start us, length us, event | category | flops | bytes accessed | tf_op | source)
XLA Modules:
  0.0 1055.5 jit_solution(14751792335652611730)
XLA Ops:
  23.5 33.3 %all_gather.30 = bf16[128,512]{0,1:T(8,128)(2,1)} all-gather(bf16[128,64]{0,1:T(8,128)(2,1)S(1)} %copy-done.28), channel_id=1, replica_groups=mesh['fsdp'=8,'tp'=4] {'fsdp'}, dimensions={1}, use_global_device_ids=true | all-gather | bytes 147456 | tf_op jit(solution)/shard_map/all_gather | solution.py:157
  56.8 31.0 %all_gather.29 = bf16[512,3,128]{2,0,1:T(8,128)(2,1)S(1)} all-gather(bf16[64,3,128]{2,0,1:T(8,128)(2,1)S(1)} %copy-done.26), channel_id=1, replica_groups=mesh['fsdp'=8,'tp'=4] {'fsdp'}, dimensions={0}, use_global_device_ids=true | all-gather | bytes 442368 | tf_op jit(solution)/shard_map/all_gather | solution.py:156
  97.2 209.4 %while.30 = (s32[]{:T(128)}, f32[8,512,2,64]{1,0,3,2:T(8,128)}, f32[8,2,512]{2,1,0:T(2,128)S(1)}, s32[8,512]{1,0:T(8,128)S(1)}, s32[1,4096]{1,0:T(1,128)S(1)}, /...) while((s32[]{:T(128)}, f32[8,512,2,64]{1,0,3,2:T(8,128)}, ...), condition=%wide.region_5.6_spmd.clone.clone, body=%wide.region_2.5_spmd.clone.clone.sunk | while | flops 1136655872 | bytes 62323844 | solution.py:73
  315.6 45.1 %reduce-scatter.5.cloned.1.call-done = bf16[1024,512]{1,0:T(8,128)(2,1)} async-done(((bf16[4096,512]{1,0:T(8,128)(2,1)}), bf16[1024,512]{1,0:T(8,128)(2,1)}) %reduce-scatter.5.cloned.1.call-update) | async-done | bytes 1048592 | tf_op jit(solution)/shard_map/reduce_scatter | solution.py:193
  367.3 33.5 %all_gather.32 = bf16[512,512]{1,0:T(8,128)(2,1)} all-gather(bf16[64,512]{1,0:T(8,128)(2,1)S(1)} %copy-done.24), channel_id=1, replica_groups=mesh['fsdp'=8,'tp'=4] {'fsdp'}, dimensions={0}, use_global_device_ids=true | all-gather | bytes 589824 | tf_op jit(solution)/shard_map/all_gather | solution.py:158
  400.8 33.5 %all_gather.33 = bf16[512,512]{0,1:T(8,128)(2,1)} all-gather(bf16[512,64]{0,1:T(8,128)(2,1)S(1)} %copy-done.25), channel_id=1, replica_groups=mesh['fsdp'=8,'tp'=4] {'fsdp'}, dimensions={1}, use_global_device_ids=true | all-gather | bytes 589824 | tf_op jit(solution)/shard_map/all_gather | solution.py:159
  434.3 10.4 multiply_convert_fusion.2
  444.7 9.8 convert_reduce_fusion
  468.5 37.5 %reduce-scatter.9.cloned.1.call-done = bf16[1024,512]{1,0:T(8,128)(2,1)} async-done(((bf16[4096,512]{1,0:T(8,128)(2,1)}), bf16[1024,512]{1,0:T(8,128)(2,1)}) %reduce-scatter.9.cloned.1.call-update) | async-done | bytes 1048592 | tf_op jit(solution)/shard_map/reduce_scatter | solution.py:225
  509.2 43.7 %reduce-scatter.7.cloned.1.call-done = bf16[1024,512]{1,0:T(8,128)(2,1)} async-done(((bf16[4096,512]{1,0:T(8,128)(2,1)}), bf16[1024,512]{1,0:T(8,128)(2,1)}) %reduce-scatter.7.cloned.1.call-update) | async-done | bytes 1048592 | tf_op jit(solution)/shard_map/reduce_scatter | solution.py:211
  557.9 34.5 %all-gather.11.cloned.1.call-done = bf16[4096,512]{1,0:T(8,128)(2,1)} async-done(((bf16[1024,512]{1,0:T(8,128)(2,1)}), bf16[4096,512]{1,0:T(8,128)(2,1)}) %all-gather.11.cloned.1.call-update) | async-done | bytes 4194320 | tf_op jit(solution)/shard_map/all_gather | solution.py:244
  602.7 300.8 %while.31 = (s32[]{:T(128)}, f32[4096,2,64]{0,2,1:T(8,128)S(1)}, f32[4096,2,64]{0,2,1:T(8,128)}, bf16[8,512,2,64]{1,3,2,0:T(8,128)(2,1)}, bf16[8,512,2,64]{1,3,2...) while((s32[]{:T(128)}, f32[4096,2,64]{0,2,1:T(8,128)S(1)}, ...), condition=%wide.region_15.16_spmd.clone.clone, body=%wide.region_14.15_spmd.clone.clone.sunk | while | flops 2745172480 | bytes 161287376 | solution.py:122
  623.5 10.5 multiply_convert_fusion.7
  661.1 10.5 multiply_convert_fusion.7
  698.6 10.5 multiply_convert_fusion.7
  736.2 10.5 multiply_convert_fusion.7
  773.8 10.5 multiply_convert_fusion.7
  811.4 10.5 multiply_convert_fusion.7
  849.0 10.5 multiply_convert_fusion.7
  886.6 10.5 multiply_convert_fusion.7
  942.9 8.3 all-to-all-done.3
  957.4 12.2 %all-to-all-done.2 = bf16[8,64,512]{2,1,0:T(8,128)(2,1)} async-done(((bf16[8,64,512]{2,1,0:T(8,128)(2,1)}), bf16[8,64,512]{2,1,0:T(8,128)(2,1)}, u32[]{:S(2)}, u32[]{:S(2)}) %all-to-all-start.2) | async-done | bytes 524320 | tf_op jit(solution)/shard_map/all_to_all | solution.py:21
  995.2 7.6 all-to-all-done
  1006.0 39.5 %all-reduce = (f32[512]{0:T(512)}, f32[512]{0:T(512)}, f32[2,512]{1,0:T(2,128)}, f32[512]{0:T(512)}, f32[512]{0:T(512)}, /*index=5*/f32[512]{0:T(512)}, f32[2048]{0:T(1024)}, f32[512]{0:T(512)}) all-reduce(f32[512]{0:T(512)S(1)} %get-tuple-element.300, ...), channel_id=1, replica_groups=mesh['fsdp'=8,'tp'=4] {'fsdp','tp'}, use_global_device_ids=true, to_apply=%region_20.21 | all-reduce | flops 6144 | bytes 49152 | tf_op jit(solution)/shard_map/psum | solution.py:291
  (343 shorter events, 574.5 us)
Async XLA Ops:
  7.2 16.3 %copy-start.28 = (bf16[128,64]{0,1:T(8,128)(2,1)S(1)}, bf16[128,64]{0,1:T(8,128)(2,1)}, u32[]{:S(2)}) copy-start(bf16[128,64]{0,1:T(8,128)(2,1)} %param.26) | copy-start | bytes 49156
  7.2 49.6 %copy-start.26 = (bf16[64,3,128]{2,0,1:T(8,128)(2,1)S(1)}, bf16[64,3,128]{2,0,1:T(8,128)(2,1)}, u32[]{:S(2)}) copy-start(bf16[64,3,128]{2,0,1:T(8,128)(2,1)} %param.24) | copy-start | bytes 147460
  7.2 81.2 %all-gather.5.cloned.1.call-start = ((), (), s32[]{:S(2)}) async-start(), calls=%async_computation.8 | async-start | bytes 5242880 | tf_op jit(solution)/shard_map/all_gather | solution.py:171
  15.1 345.6 %reduce-scatter.5.cloned.1.call-start = ((), (), s32[]{:S(2)}) async-start(), calls=%async_computation.9 | async-start | bytes 5242880 | tf_op jit(solution)/shard_map/reduce_scatter | solution.py:193
  314.9 45.9 %copy-start.1 = (bf16[1024,512]{1,0:T(8,128)(2,1)S(1)}, bf16[1024,512]{1,0:T(8,128)(2,1)}, u32[]{:S(2)}) copy-start(bf16[1024,512]{1,0:T(8,128)(2,1)} %param.19) | copy-start | bytes 3145732
  314.9 119.4 %all-gather.7.cloned.1.call-start = ((), (), s32[]{:S(2)}) async-start(), calls=%async_computation.10 | async-start | bytes 5242880 | tf_op jit(solution)/shard_map/all_gather | solution.py:204
  364.3 36.5 %copy-start.25 = (bf16[512,64]{0,1:T(8,128)(2,1)S(1)}, bf16[512,64]{0,1:T(8,128)(2,1)}, u32[]{:S(2)}) copy-start(bf16[512,64]{0,1:T(8,128)(2,1)} %param.32) | copy-start | bytes 196612
  365.9 78.8 %all-gather.9.cloned.1.call-start = ((), (), s32[]{:S(2)}) async-start(), calls=%async_computation.12 | async-start | bytes 5242880 | tf_op jit(solution)/shard_map/all_gather | solution.py:217
  366.5 139.4 %reduce-scatter.9.cloned.1.call-start = ((), (), s32[]{:S(2)}) async-start(), calls=%async_computation.13 | async-start | bytes 5242880 | tf_op jit(solution)/shard_map/reduce_scatter | solution.py:225
  461.0 91.9 %reduce-scatter.7.cloned.1.call-start = ((), (), s32[]{:S(2)}) async-start(), calls=%async_computation.11 | async-start | bytes 5242880 | tf_op jit(solution)/shard_map/reduce_scatter | solution.py:211
  467.8 124.6 %all-gather.11.cloned.1.call-start = ((), (), s32[]{:S(2)}) async-start(), calls=%async_computation.14 | async-start | bytes 5242880 | tf_op jit(solution)/shard_map/all_gather | solution.py:244
  557.8 445.7 %reduce-scatter.11.cloned.1.call-start = ((), (), s32[]{:S(2)}) async-start(), calls=%async_computation.15 | async-start | bytes 5242880 | tf_op jit(solution)/shard_map/reduce_scatter | solution.py:261
  930.6 20.5 %all-to-all-start.3 = ((bf16[8,512,64]{1,2,0:T(8,128)(2,1)}), bf16[8,512,64]{1,2,0:T(8,128)(2,1)}, u32[]{:S(2)}, u32[]{:S(2)}) async-start(bf16[8,512,64]{1,2,0:T(8,128)(2,1)} %bitcast.13), calls=%async_computation.7 | async-start | bytes 1048576 | tf_op jit(solution)/shard_map/all_to_all | solution.py:21
  936.2 19.2 %copy-start.31 = (f32[512]{0:T(512)S(1)}, f32[512]{0:T(512)}, u32[]{:S(2)}) copy-start(f32[512]{0:T(512)} %get-tuple-element.377) | copy-start | bytes 6148
  936.2 35.2 %copy-start.19 = (f32[1,4096]{1,0:T(1,128)S(1)}, f32[1,4096]{1,0:T(1,128)}, u32[]{:S(2)}) copy-start(f32[1,4096]{1,0:T(1,128)} %compare_convert_fusion) | copy-start | bytes 49156
  942.9 28.5 %copy-start.4 = (f32[16,8,8,512]{3,1,2,0:T(8,128)S(1)}, f32[16,8,8,512]{3,1,2,0:T(8,128)}, u32[]{:S(2)}) copy-start(f32[16,8,8,512]{3,1,2,0:T(8,128)} %copy-done.3) | copy-start | bytes 6291460
  951.2 18.4 %all-to-all-start.2 = ((bf16[8,64,512]{2,1,0:T(8,128)(2,1)}), bf16[8,64,512]{2,1,0:T(8,128)(2,1)}, u32[]{:S(2)}, u32[]{:S(2)}) async-start(bf16[8,64,512]{2,1,0:T(8,128)(2,1)} %bitcast.175), calls=%async_computation.6 | async-start | bytes 1048576 | tf_op jit(solution)/shard_map/all_to_all | solution.py:21
  975.0 11.0 %all-to-all-start.1 = ((bf16[8,128,64]{1,2,0:T(8,128)(2,1)}), bf16[8,128,64]{1,2,0:T(8,128)(2,1)S(1)}, u32[]{:S(2)}, u32[]{:S(2)}) async-start(bf16[8,128,64]{1,2,0:T(8,128)(2,1)} %bitcast.10), calls=%async_computation.5 | async-start | bytes 262144 | tf_op jit(solution)/shard_map/all_to_all | solution.py:21
  978.7 13.0 %copy-start.11 = (bf16[4096,1,128]{2,0,1:T(8,128)(2,1)S(1)}, bf16[4096,1,128]{2,0,1:T(8,128)(2,1)}, u32[]{:S(2)}) copy-start(bf16[4096,1,128]{2,0,1:T(8,128)(2,1)} %copy-done.10) | copy-start | bytes 3145732
  986.7 16.1 %all-to-all-start = ((bf16[8,64,3,128]{3,1,2,0:T(8,128)(2,1)}), bf16[8,64,3,128]{3,1,2,0:T(8,128)(2,1)S(1)}, u32[]{:S(2)}, u32[]{:S(2)}) async-start(bf16[8,64,3,128]{3,1,2,0:T(8,128)(2,1)} %copy.57), calls=%async_computation.4 | async-start | bytes 786432 | tf_op jit(solution)/shard_map/all_to_all | solution.py:21
  991.7 11.8 %copy-start.2 = (bf16[1024,512]{1,0:T(8,128)(2,1)S(1)}, bf16[1024,512]{1,0:T(8,128)(2,1)}, u32[]{:S(2)}) copy-start(bf16[1024,512]{1,0:T(8,128)(2,1)} %param.19) | copy-start | bytes 3145732
  991.7 11.8 %copy-start.21 = (f32[1024]{0:T(1024)S(1)}, f32[1024]{0:T(1024)}, u32[]{:S(2)}) copy-start(f32[1024]{0:T(1024)} %copy-done.20) | copy-start | bytes 12292
  991.7 11.8 %copy-start.23 = (f32[1024]{0:T(1024)S(1)}, f32[1024]{0:T(1024)}, u32[]{:S(2)}) copy-start(f32[1024]{0:T(1024)} %copy-done.22) | copy-start | bytes 12292
  993.4 52.1 %copy-start.6 = (f32[1024,512]{1,0:T(8,128)S(1)}, f32[1024,512]{1,0:T(8,128)}, u32[]{:S(2)}) copy-start(f32[1024,512]{1,0:T(8,128)} %get-tuple-element.362) | copy-start | bytes 6291460
  (32 other events, 125.5 us)
Sparse Core Ops, SparseCore 0:
  15.2 37.1 all-gather.4
  315.0 45.6 reduce-scatter.4
  366.0 34.4 all-gather.6
  401.9 34.4 all-gather.8
  461.1 44.7 reduce-scatter.8
  508.3 44.5 reduce-scatter.6
  557.9 34.4 all-gather.10
  924.1 44.5 reduce-scatter.10
where the time goes:
time: 1060 us
  matrix products  373 us (35%)
  waiting for transfers between devices  191 us (18%)
  blocking collectives  177 us (17%)
  other arithmetic  147 us (14%)
  local copies, waits for them, and re-layouts  132 us (12%)
  starting transfers between devices  18.6 us (2%)
  between operations  15.2 us (1%)
    dot_general x8, matrix products, one_block(): jnp.einsum('qhe,khe->hqk', g_blk, values_all, preferred_element_type=jnp....  84.2 us
    and x16, other arithmetic, allowed(): return same_doc & causal & living  69.2 us
    dot_general x8, matrix products, one_block(): jnp.einsum('hqk,qhe->khe', softmax_f.astype(jnp.bfloat16), g_blk, preferr...  60.4 us
    dot_general x16, matrix products, one_block(): jnp.einsum('qhe,khe->hqk', q_blk, keys_all, preferred_element_type=jnp.fl...  56.1 us
    dot_general x8, matrix products, one_block(): jnp.einsum('hqk,khe->qhe', softmax_w, values_all, preferred_element_type=...  54.3 us
    dynamic_update_slice x16, local copies, waits for them, and re-layouts, attend(): lax.map(one_block, (queries.reshape(blocks, block_rows, heads_here, head_...  53 us
    while x16, local copies, waits for them, and re-layouts  45.6 us
    reduce_scatter x1, waiting for transfers between devices, local(): lax.psum_scatter(jnp.dot(attn_low, out_full, preferred_element_type=jnp.f...  45.1 us
  transfers between devices with their start and end apart: 12, of which 8 were waited for; matrix products, arithmetic and copies ran while one was open for 5% of the time, Pallas kernels for 0%

commit v1 on v0

--- a/solution.py
+++ b/solution.py
@@ -8,6 +8,15 @@
 epsilon = 1e-05
 gelu_slope = 1.702
 masked_score = -1e30
+
+
+def _order_goods(x_local, ndim_at):
+    x_local = jnp.moveaxis(x_local, 0, ndim_at)
+    arr_out = x_local.shape
+    base_arr = x_local.reshape(
+        *arr_out[:ndim_at], arr_out[ndim_at] * arr_out[ndim_at + 1], *arr_out[ndim_at + 2 :]
+    )
+    return base_arr
 
 
 def split_up(value, dim, peers):
@@ -241,7 +250,20 @@
     grad_hidden_low = grad_hidden.astype(jnp.bfloat16)
     out_bias_part = jnp.sum(grad_hidden_low.astype(jnp.float32), axis=0)
     proj_bias_part = jnp.sum(resid_grad, axis=0)
-    seq_grad = lax.all_gather(grad_hidden_low, "tp", axis=0, tiled=True)
+
+    def perform_modes(along_dim, axis_name, mine_x):
+        world = lax.axis_size(axis_name)
+        gallery = [(ii, (ii + 1) % world) for ii in range(world)]
+        store = [mine_x]
+        while len(store) < world:
+            answer = lax.ppermute(store[-1], axis_name, gallery)
+            store.append(answer)
+        outcome_arr = lax.axis_index(axis_name)
+        store = jnp.stack(store)[(outcome_arr - jnp.arange(world)) % world]
+        moved = _order_goods(store, along_dim)
+        return moved
+
+    seq_grad = perform_modes(0, "tp", mine_x=grad_hidden_low)
     out_w_grad = jnp.einsum("sc,sd->cd", attn_low, seq_grad, preferred_element_type=jnp.float32)
     grad_attn = jnp.einsum("sd,cd->sc", seq_grad, out_full, preferred_element_type=jnp.float32)
     grad_attn_low = (

time: 1060 us -> 1030 us (0.972)
  local copies, waits for them, and re-layouts: 132 us -> 85.7 us
    dynamic_update_slice x16 -> x0, local copies, waits for them, and re-layouts: 53 us -> none  [attend(): lax.map(one_block, (queries.reshape(blocks, block_rows, heads_here, head_...]
    ppermute x0 -> x3, waiting for transfers between devices: none -> 41.4 us  [perform_modes(): answer = lax.ppermute(store[-1], axis_name, gallery)]
    all_gather x1 -> x0, waiting for transfers between devices: 34.5 us -> none  [local(): seq_grad = lax.all_gather(grad_hidden_low, 'tp', axis=0, tiled=True)]
    while x16 -> x17, local copies, waits for them, and re-layouts: 45.6 us -> 46.9 us
  transfers between devices with their start and end apart: 12 -> 14, of which waited for: 8 -> 10; matrix products, arithmetic and copies ran while one was open for 5% -> 6% of each run, Pallas kernels for 0% -> 0%
where the time goes in v1:
time: 1030 us; the launch traced here: 1020 us
  matrix products  380 us (37%)
  waiting for transfers between devices  192 us (19%)
  blocking collectives  177 us (17%)
  other arithmetic  154 us (15%)
  local copies, waits for them, and re-layouts  85.7 us (8%)
  starting transfers between devices  18 us (2%)
  between operations  15.1 us (1%)
    dot_general x8, matrix products, one_block(): jnp.einsum('qhe,khe->hqk', g_blk, values_all, preferred_element_type=jnp....  84.2 us
    and x16, other arithmetic, allowed(): return same_doc & causal & living  69.2 us
    dot_general x16, matrix products, one_block(): jnp.einsum('qhe,khe->hqk', q_blk, keys_all, preferred_element_type=jnp.fl...  63.3 us
    dot_general x8, matrix products, one_block(): jnp.einsum('hqk,qhe->khe', softmax_f.astype(jnp.bfloat16), g_blk, preferr...  60.4 us
    dot_general x8, matrix products, one_block(): jnp.einsum('hqk,khe->qhe', softmax_w, values_all, preferred_element_type=...  54.3 us
    while x16, local copies, waits for them, and re-layouts  45.6 us
    reduce_scatter x1, waiting for transfers between devices, local(): lax.psum_scatter(jnp.dot(attn_low, out_full, preferred_element_type=jnp.f...  45.1 us
    reduce_scatter x1, waiting for transfers between devices, local(): lax.psum_scatter(jnp.dot(act_low, proj_full, preferred_element_type=jnp.f...  43.7 us
  transfers between devices with their start and end apart: 14, of which 10 were waited for; matrix products, arithmetic and copies ran while one was open for 6% of the time, Pallas kernels for 0%

profile of v1, /device:TPU:0, one launch (start us, length us, event | category | flops | bytes accessed | tf_op | source)
XLA Modules:
  0.0 1024.3 jit_solution(2278450643396322352)
XLA Ops:
  23.5 33.3 %all_gather.27 = bf16[128,512]{0,1:T(8,128)(2,1)} all-gather(bf16[128,64]{0,1:T(8,128)(2,1)S(1)} %copy-done.30), channel_id=1, replica_groups=mesh['fsdp'=8,'tp'=4] {'fsdp'}, dimensions={1}, use_global_device_ids=true | all-gather | bytes 147456 | tf_op jit(solution)/shard_map/all_gather | solution.py:166
  56.8 31.0 %all_gather.26 = bf16[512,3,128]{2,0,1:T(8,128)(2,1)S(1)} all-gather(bf16[64,3,128]{2,0,1:T(8,128)(2,1)S(1)} %copy-done.28), channel_id=1, replica_groups=mesh['fsdp'=8,'tp'=4] {'fsdp'}, dimensions={0}, use_global_device_ids=true | all-gather | bytes 442368 | tf_op jit(solution)/shard_map/all_gather | solution.py:165
  98.2 163.7 %while.32 = (s32[]{:T(128)}, f32[8,512,2,64]{1,3,2,0:T(8,128)S(1)}, f32[8,2,512]{2,1,0:T(2,128)S(1)}, s32[8,512]{1,0:T(8,128)S(1)}, s32[1,4096]{1,0:T(1,128)S(1)...) while((s32[]{:T(128)}, f32[8,512,2,64]{1,3,2,0:T(8,128)S(1)}, ...), condition=%wide.region_5.6_spmd.clone.clone.clone, body=%wide.region_2.5_spmd.clone.clone.sunk.clone | while | flops 1136655872 | bytes 61275252 | solution.py:82
  268.7 45.1 %reduce-scatter.5.cloned.1.call-done = bf16[1024,512]{1,0:T(8,128)(2,1)} async-done(((bf16[4096,512]{1,0:T(8,128)(2,1)}), bf16[1024,512]{1,0:T(8,128)(2,1)}) %reduce-scatter.5.cloned.1.call-update) | async-done | bytes 1048592 | tf_op jit(solution)/shard_map/reduce_scatter | solution.py:202
  320.4 33.5 %all_gather.29 = bf16[512,512]{1,0:T(8,128)(2,1)} all-gather(bf16[64,512]{1,0:T(8,128)(2,1)S(1)} %copy-done.26), channel_id=1, replica_groups=mesh['fsdp'=8,'tp'=4] {'fsdp'}, dimensions={0}, use_global_device_ids=true | all-gather | bytes 589824 | tf_op jit(solution)/shard_map/all_gather | solution.py:167
  354.0 33.5 %all_gather.30 = bf16[512,512]{0,1:T(8,128)(2,1)} all-gather(bf16[512,64]{0,1:T(8,128)(2,1)S(1)} %copy-done.27), channel_id=1, replica_groups=mesh['fsdp'=8,'tp'=4] {'fsdp'}, dimensions={1}, use_global_device_ids=true | all-gather | bytes 589824 | tf_op jit(solution)/shard_map/all_gather | solution.py:168
  387.5 10.4 %multiply_convert_fusion.2 = (bf16[4096,512]{1,0:T(8,128)(2,1)}, f32[4096,512]{1,0:T(8,128)}) fusion(f32[512]{0:T(512)S(1)} %dynamic-slice_convert_fusion, bf16[4096,512]{1,0:T(8,128)(2,1)} %all-gather.6.cloned.1.call-done, bf16[512,512]{1,0:T(8,128)(2,1)} %all_gather.29), kind=kOutput, calls=%fused_computation.66 | convolution fusion | flops 2162163712 | bytes 17303552 | tf_op jit(solution)/shard_map/dot_general | solution.py:215
  397.9 9.8 convert_reduce_fusion
  421.6 37.4 %reduce-scatter.9.cloned.1.call-done = bf16[1024,512]{1,0:T(8,128)(2,1)} async-done(((bf16[4096,512]{1,0:T(8,128)(2,1)}), bf16[1024,512]{1,0:T(8,128)(2,1)}) %reduce-scatter.9.cloned.1.call-update) | async-done | bytes 1048592 | tf_op jit(solution)/shard_map/reduce_scatter | solution.py:234
  462.3 43.7 %reduce-scatter.7.cloned.1.call-done = bf16[1024,512]{1,0:T(8,128)(2,1)} async-done(((bf16[4096,512]{1,0:T(8,128)(2,1)}), bf16[1024,512]{1,0:T(8,128)(2,1)}) %reduce-scatter.7.cloned.1.call-update) | async-done | bytes 1048592 | tf_op jit(solution)/shard_map/reduce_scatter | solution.py:220
  511.7 14.2 %collective-permute-done = bf16[1024,512]{1,0:T(8,128)(2,1)S(1)} collective-permute-done((bf16[1024,512]{1,0:T(8,128)(2,1)S(1)}, bf16[1024,512]{1,0:T(8,128)(2,1)S(1)}, u32[]{:S(2)}, u32[]{:S(2)}) %collective-permute-start) | collective-permute-done | bytes 1048608 | tf_op jit(solution)/shard_map/ppermute | solution.py:259
  526.8 14.3 %collective-permute-done.1 = bf16[1024,512]{1,0:T(8,128)(2,1)} collective-permute-done((bf16[1024,512]{1,0:T(8,128)(2,1)S(1)}, bf16[1024,512]{1,0:T(8,128)(2,1)}, u32[]{:S(2)}, u32[]{:S(2)}) %collective-permute-start.1) | collective-permute-done | bytes 1048608 | tf_op jit(solution)/shard_map/ppermute | solution.py:259
  542.9 12.8 %collective-permute-done.2 = bf16[1024,512]{1,0:T(8,128)(2,1)} collective-permute-done((bf16[1024,512]{1,0:T(8,128)(2,1)}, bf16[1024,512]{1,0:T(8,128)(2,1)}, u32[]{:S(2)}, u32[]{:S(2)}) %collective-permute-start.2) | collective-permute-done | bytes 1048608 | tf_op jit(solution)/shard_map/ppermute | solution.py:259
  575.5 300.8 %while.33 = (s32[]{:T(128)}, f32[4096,2,64]{0,2,1:T(8,128)S(1)}, f32[4096,2,64]{0,2,1:T(8,128)}, bf16[8,512,2,64]{1,3,2,0:T(8,128)(2,1)}, bf16[8,512,2,64]{1,3,2...) while((s32[]{:T(128)}, f32[4096,2,64]{0,2,1:T(8,128)S(1)}, ...), condition=%wide.region_15.16_spmd.clone.clone.clone, body=%wide.region_14.15_spmd.clone.clone.sunk.clone | while | flops 2745172480 | bytes 161287376 | solution.py:131
  596.3 10.5 %multiply_convert_fusion.8 = bf16[2,512,4096]{2,1,0:T(8,128)(2,1)S(1)} fusion(f32[2,512,4096]{2,1,0:T(8,128)} %copy-done, bf16[4096,2,64]{0,2,1:T(8,128)(2,1)} %get-tuple-element.648, f32[2,512]{1,0:T(2,128)S(1)} %bitcast.229, f32[2,512]{1,0:T(2,128)S(1)} %dynamic-slice_bitcast_fusion.3, pred[512,4096]{1,0:T(8,128)(4,1)S(1)} %fusion.171, ...), kind=kOutput, calls=%fused_computation.26.clone.1.clone | convolution fusion | flops 566231040 | bytes 28450820 | tf_op jit(solution)/shard_map/while/body/eval_jaxpr/qhe,khe->hqk/dot_general | solution.py:110
  633.9 10.5 %multiply_convert_fusion.8 = bf16[2,512,4096]{2,1,0:T(8,128)(2,1)S(1)} fusion(f32[2,512,4096]{2,1,0:T(8,128)} %copy-done, bf16[4096,2,64]{0,2,1:T(8,128)(2,1)} %get-tuple-element.648, f32[2,512]{1,0:T(2,128)S(1)} %bitcast.229, f32[2,512]{1,0:T(2,128)S(1)} %dynamic-slice_bitcast_fusion.3, pred[512,4096]{1,0:T(8,128)(4,1)S(1)} %fusion.171, ...), kind=kOutput, calls=%fused_computation.26.clone.1.clone | convolution fusion | flops 566231040 | bytes 28450820 | tf_op jit(solution)/shard_map/while/body/eval_jaxpr/qhe,khe->hqk/dot_general | solution.py:110
  671.5 10.5 %multiply_convert_fusion.8 = bf16[2,512,4096]{2,1,0:T(8,128)(2,1)S(1)} fusion(f32[2,512,4096]{2,1,0:T(8,128)} %copy-done, bf16[4096,2,64]{0,2,1:T(8,128)(2,1)} %get-tuple-element.648, f32[2,512]{1,0:T(2,128)S(1)} %bitcast.229, f32[2,512]{1,0:T(2,128)S(1)} %dynamic-slice_bitcast_fusion.3, pred[512,4096]{1,0:T(8,128)(4,1)S(1)} %fusion.171, ...), kind=kOutput, calls=%fused_computation.26.clone.1.clone | convolution fusion | flops 566231040 | bytes 28450820 | tf_op jit(solution)/shard_map/while/body/eval_jaxpr/qhe,khe->hqk/dot_general | solution.py:110
  709.1 10.5 %multiply_convert_fusion.8 = bf16[2,512,4096]{2,1,0:T(8,128)(2,1)S(1)} fusion(f32[2,512,4096]{2,1,0:T(8,128)} %copy-done, bf16[4096,2,64]{0,2,1:T(8,128)(2,1)} %get-tuple-element.648, f32[2,512]{1,0:T(2,128)S(1)} %bitcast.229, f32[2,512]{1,0:T(2,128)S(1)} %dynamic-slice_bitcast_fusion.3, pred[512,4096]{1,0:T(8,128)(4,1)S(1)} %fusion.171, ...), kind=kOutput, calls=%fused_computation.26.clone.1.clone | convolution fusion | flops 566231040 | bytes 28450820 | tf_op jit(solution)/shard_map/while/body/eval_jaxpr/qhe,khe->hqk/dot_general | solution.py:110
  746.7 10.5 %multiply_convert_fusion.8 = bf16[2,512,4096]{2,1,0:T(8,128)(2,1)S(1)} fusion(f32[2,512,4096]{2,1,0:T(8,128)} %copy-done, bf16[4096,2,64]{0,2,1:T(8,128)(2,1)} %get-tuple-element.648, f32[2,512]{1,0:T(2,128)S(1)} %bitcast.229, f32[2,512]{1,0:T(2,128)S(1)} %dynamic-slice_bitcast_fusion.3, pred[512,4096]{1,0:T(8,128)(4,1)S(1)} %fusion.171, ...), kind=kOutput, calls=%fused_computation.26.clone.1.clone | convolution fusion | flops 566231040 | bytes 28450820 | tf_op jit(solution)/shard_map/while/body/eval_jaxpr/qhe,khe->hqk/dot_general | solution.py:110
  784.3 10.5 %multiply_convert_fusion.8 = bf16[2,512,4096]{2,1,0:T(8,128)(2,1)S(1)} fusion(f32[2,512,4096]{2,1,0:T(8,128)} %copy-done, bf16[4096,2,64]{0,2,1:T(8,128)(2,1)} %get-tuple-element.648, f32[2,512]{1,0:T(2,128)S(1)} %bitcast.229, f32[2,512]{1,0:T(2,128)S(1)} %dynamic-slice_bitcast_fusion.3, pred[512,4096]{1,0:T(8,128)(4,1)S(1)} %fusion.171, ...), kind=kOutput, calls=%fused_computation.26.clone.1.clone | convolution fusion | flops 566231040 | bytes 28450820 | tf_op jit(solution)/shard_map/while/body/eval_jaxpr/qhe,khe->hqk/dot_general | solution.py:110
  821.9 10.5 %multiply_convert_fusion.8 = bf16[2,512,4096]{2,1,0:T(8,128)(2,1)S(1)} fusion(f32[2,512,4096]{2,1,0:T(8,128)} %copy-done, bf16[4096,2,64]{0,2,1:T(8,128)(2,1)} %get-tuple-element.648, f32[2,512]{1,0:T(2,128)S(1)} %bitcast.229, f32[2,512]{1,0:T(2,128)S(1)} %dynamic-slice_bitcast_fusion.3, pred[512,4096]{1,0:T(8,128)(4,1)S(1)} %fusion.171, ...), kind=kOutput, calls=%fused_computation.26.clone.1.clone | convolution fusion | flops 566231040 | bytes 28450820 | tf_op jit(solution)/shard_map/while/body/eval_jaxpr/qhe,khe->hqk/dot_general | solution.py:110
  859.5 10.5 %multiply_convert_fusion.8 = bf16[2,512,4096]{2,1,0:T(8,128)(2,1)S(1)} fusion(f32[2,512,4096]{2,1,0:T(8,128)} %copy-done, bf16[4096,2,64]{0,2,1:T(8,128)(2,1)} %get-tuple-element.648, f32[2,512]{1,0:T(2,128)S(1)} %bitcast.229, f32[2,512]{1,0:T(2,128)S(1)} %dynamic-slice_bitcast_fusion.3, pred[512,4096]{1,0:T(8,128)(4,1)S(1)} %fusion.171, ...), kind=kOutput, calls=%fused_computation.26.clone.1.clone | convolution fusion | flops 566231040 | bytes 28450820 | tf_op jit(solution)/shard_map/while/body/eval_jaxpr/qhe,khe->hqk/dot_general | solution.py:110
  930.4 9.1 all-to-all-done.2
  974.8 39.5 %all-reduce = (f32[512]{0:T(512)}, f32[512]{0:T(512)}, f32[2,512]{1,0:T(2,128)}, f32[512]{0:T(512)}, f32[512]{0:T(512)}, /*index=5*/f32[512]{0:T(512)}, f32[2048]{0:T(1024)}, f32[512]{0:T(512)}) all-reduce(f32[512]{0:T(512)S(1)} %get-tuple-element.300, ...), channel_id=1, replica_groups=mesh['fsdp'=8,'tp'=4] {'fsdp','tp'}, use_global_device_ids=true, to_apply=%region_20.21 | all-reduce | flops 6144 | bytes 49152 | tf_op jit(solution)/shard_map/psum | solution.py:313
  (342 shorter events, 555.4 us)
Async XLA Ops:
  7.2 16.3 %copy-start.30 = (bf16[128,64]{0,1:T(8,128)(2,1)S(1)}, bf16[128,64]{0,1:T(8,128)(2,1)}, u32[]{:S(2)}) copy-start(bf16[128,64]{0,1:T(8,128)(2,1)} %param.26) | copy-start | bytes 49156
  7.2 49.6 %copy-start.28 = (bf16[64,3,128]{2,0,1:T(8,128)(2,1)S(1)}, bf16[64,3,128]{2,0,1:T(8,128)(2,1)}, u32[]{:S(2)}) copy-start(bf16[64,3,128]{2,0,1:T(8,128)(2,1)} %param.24) | copy-start | bytes 147460
  7.2 81.2 %all-gather.4.cloned.1.call-start = ((), (), s32[]{:S(2)}) async-start(), calls=%async_computation.8 | async-start | bytes 5242880 | tf_op jit(solution)/shard_map/all_gather | solution.py:180
  15.1 298.8 %reduce-scatter.5.cloned.1.call-start = ((), (), s32[]{:S(2)}) async-start(), calls=%async_computation.9 | async-start | bytes 5242880 | tf_op jit(solution)/shard_map/reduce_scatter | solution.py:202
  268.0 45.9 %copy-start.1 = (bf16[1024,512]{1,0:T(8,128)(2,1)S(1)}, bf16[1024,512]{1,0:T(8,128)(2,1)}, u32[]{:S(2)}) copy-start(bf16[1024,512]{1,0:T(8,128)(2,1)} %param.19) | copy-start | bytes 3145732
  268.0 119.5 %all-gather.6.cloned.1.call-start = ((), (), s32[]{:S(2)}) async-start(), calls=%async_computation.10 | async-start | bytes 5242880 | tf_op jit(solution)/shard_map/all_gather | solution.py:213
  317.4 36.6 %copy-start.27 = (bf16[512,64]{0,1:T(8,128)(2,1)S(1)}, bf16[512,64]{0,1:T(8,128)(2,1)}, u32[]{:S(2)}) copy-start(bf16[512,64]{0,1:T(8,128)(2,1)} %param.32) | copy-start | bytes 196612
  319.0 78.9 %all-gather.8.cloned.1.call-start = ((), (), s32[]{:S(2)}) async-start(), calls=%async_computation.12 | async-start | bytes 5242880 | tf_op jit(solution)/shard_map/all_gather | solution.py:226
  319.6 139.4 %reduce-scatter.9.cloned.1.call-start = ((), (), s32[]{:S(2)}) async-start(), calls=%async_computation.13 | async-start | bytes 5242880 | tf_op jit(solution)/shard_map/reduce_scatter | solution.py:234
  397.9 11.8 %copy-start.17 = (bf16[512,512]{1,0:T(8,128)(2,1)S(1)}, bf16[512,512]{1,0:T(8,128)(2,1)}, u32[]{:S(2)}) copy-start(bf16[512,512]{1,0:T(8,128)(2,1)} %all_gather.29) | copy-start | bytes 1572868
  414.2 91.8 %reduce-scatter.7.cloned.1.call-start = ((), (), s32[]{:S(2)}) async-start(), calls=%async_computation.11 | async-start | bytes 5242880 | tf_op jit(solution)/shard_map/reduce_scatter | solution.py:220
  421.0 551.3 %reduce-scatter.11.cloned.1.call-start = ((), (), s32[]{:S(2)}) async-start(), calls=%async_computation.14 | async-start | bytes 5242880 | tf_op jit(solution)/shard_map/reduce_scatter | solution.py:283
  511.7 14.2 %collective-permute-start = (bf16[1024,512]{1,0:T(8,128)(2,1)S(1)}, bf16[1024,512]{1,0:T(8,128)(2,1)S(1)}, u32[]{:S(2)}, u32[]{:S(2)}) collective-permute-start(bf16[1024,512]{1,0:T(8,128)(2,1)S(1)} %get-tuple-element.361), channel_id=1, source_target_pairs={{0,1},{1,2},{2,3},{3,0},{4,5},{5,6},{6,7},{7,4},{8,9},{9,10},{10,1... | collective-permute-start | bytes 3145736 | tf_op jit(solution)/shard_map/ppermute | solution.py:259
  526.8 14.3 %collective-permute-start.1 = (bf16[1024,512]{1,0:T(8,128)(2,1)S(1)}, bf16[1024,512]{1,0:T(8,128)(2,1)}, u32[]{:S(2)}, u32[]{:S(2)}) collective-permute-start(bf16[1024,512]{1,0:T(8,128)(2,1)S(1)} %collective-permute-done), channel_id=1, source_target_pairs={{0,1},{1,2},{2,3},{3,0},{4,5},{5,6},{6,7},{7,4},{8,9},{9,10},{10,1... | collective-permute-start | bytes 3145736 | tf_op jit(solution)/shard_map/ppermute | solution.py:259
  541.2 14.5 %collective-permute-start.2 = (bf16[1024,512]{1,0:T(8,128)(2,1)}, bf16[1024,512]{1,0:T(8,128)(2,1)}, u32[]{:S(2)}, u32[]{:S(2)}) collective-permute-start(bf16[1024,512]{1,0:T(8,128)(2,1)} %collective-permute-done.1), channel_id=1, source_target_pairs={{0,1},{1,2},{2,3},{3,0},{4,5},{5,6},{6,7},{7,4},{8,9},{9,10},{10,1... | collective-permute-start | bytes 3145736 | tf_op jit(solution)/shard_map/ppermute | solution.py:259
  903.5 18.4 %all-to-all-start.3 = ((bf16[8,512,64]{1,2,0:T(8,128)(2,1)}), bf16[8,512,64]{1,2,0:T(8,128)(2,1)}, u32[]{:S(2)}, u32[]{:S(2)}) async-start(bf16[8,512,64]{1,2,0:T(8,128)(2,1)} %bitcast.19), calls=%async_computation.7 | async-start | bytes 1048576 | tf_op jit(solution)/shard_map/all_to_all | solution.py:30
  909.0 17.1 %copy-start.6 = (f32[8,512,2,64]{1,3,2,0:T(8,128)S(1)}, f32[8,512,2,64]{1,3,2,0:T(8,128)}, u32[]{:S(2)}) copy-start(f32[8,512,2,64]{1,3,2,0:T(8,128)} %copy-done.4) | copy-start | bytes 6291460
  909.0 17.1 %copy-start.25 = (f32[8,512]{1,0:T(8,128)S(1)}, f32[8,512]{1,0:T(8,128)}, u32[]{:S(2)}) copy-start(f32[8,512]{1,0:T(8,128)} %get-tuple-element.375) | copy-start | bytes 49156
  921.9 17.5 %all-to-all-start.2 = ((bf16[8,64,512]{2,1,0:T(8,128)(2,1)}), bf16[8,64,512]{2,1,0:T(8,128)(2,1)}, u32[]{:S(2)}, u32[]{:S(2)}) async-start(bf16[8,64,512]{2,1,0:T(8,128)(2,1)} %bitcast.220), calls=%async_computation.6 | async-start | bytes 1048576 | tf_op jit(solution)/shard_map/all_to_all | solution.py:30
  930.4 18.9 %copy-start.10 = (bf16[4096,1,128]{2,0,1:T(8,128)(2,1)S(1)}, bf16[4096,1,128]{2,0,1:T(8,128)(2,1)}, u32[]{:S(2)}) copy-start(bf16[4096,1,128]{2,0,1:T(8,128)(2,1)} %copy-done.9) | copy-start | bytes 3145732
  930.4 18.9 %copy-start.11 = (bf16[4096,1,128]{2,0,1:T(8,128)(2,1)S(1)}, bf16[4096,1,128]{2,0,1:T(8,128)(2,1)}, u32[]{:S(2)}) copy-start(bf16[4096,1,128]{2,0,1:T(8,128)(2,1)} %copy.56) | copy-start | bytes 3145732
  945.2 11.3 %all-to-all-start.1 = ((bf16[8,128,64]{1,2,0:T(8,128)(2,1)}), bf16[8,128,64]{1,2,0:T(8,128)(2,1)S(1)}, u32[]{:S(2)}, u32[]{:S(2)}) async-start(bf16[8,128,64]{1,2,0:T(8,128)(2,1)} %bitcast.16), calls=%async_computation.5 | async-start | bytes 262144 | tf_op jit(solution)/shard_map/all_to_all | solution.py:30
  957.2 14.4 %all-to-all-start = ((bf16[8,64,3,128]{3,1,2,0:T(8,128)(2,1)}), bf16[8,64,3,128]{3,1,2,0:T(8,128)(2,1)S(1)}, u32[]{:S(2)}, u32[]{:S(2)}) async-start(bf16[8,64,3,128]{3,1,2,0:T(8,128)(2,1)} %copy.58), calls=%async_computation.4 | async-start | bytes 786432 | tf_op jit(solution)/shard_map/all_to_all | solution.py:30
  962.9 51.3 %copy-start.7 = (f32[1024,512]{1,0:T(8,128)S(1)}, f32[1024,512]{1,0:T(8,128)}, u32[]{:S(2)}) copy-start(f32[1024,512]{1,0:T(8,128)} %get-tuple-element.362) | copy-start | bytes 6291460
  (36 other events, 138.3 us)
Sparse Core Ops, SparseCore 0:
  15.2 37.1 all-gather.3
  268.1 45.6 reduce-scatter.4
  319.1 34.4 all-gather.5
  355.1 34.4 all-gather.7
  414.3 44.6 reduce-scatter.8
  461.4 44.5 reduce-scatter.6
  897.0 44.5 reduce-scatter.10
